TPU v7x, 128 devices: a whole 4x4x4 slice. The times are simulated.
128 devices in a mesh: seq: 32 (over y, x, z_lo), mp: 4 (over z_hi, core).
Axes of the slice: x: 4, y: 4, z: 4 (z_hi: 2, z_lo: 2; z = z_hi * 2 + z_lo), core: 2. Of those that a mesh axis runs over, the one named last changes fastest.
Arguments:
- frames: bfloat16 [768, 250, 256], P('seq'), may hold values from -7.5 to 7.5
- intra_qkv: bfloat16 [256, 3, 256], P(None, None, 'mp'), may hold values from -20 to 20
- intra_out: bfloat16 [256, 256], P('mp'), may hold values from -0.375 to 0.375
- intra_up: bfloat16 [256, 1024], P(None, 'mp'), may hold values from -0.375 to 0.375
- intra_down: bfloat16 [1024, 256], P('mp'), may hold values from -0.1875 to 0.1875
- inter_qkv: bfloat16 [256, 3, 256], P(None, None, 'mp'), may hold values from -20 to 20
- inter_out: bfloat16 [256, 256], P('mp'), may hold values from -0.375 to 0.375
- inter_up: bfloat16 [256, 1024], P(None, 'mp'), may hold values from -0.375 to 0.375
- inter_down: bfloat16 [1024, 256], P('mp'), may hold values from -0.1875 to 0.1875
Outputs:
- margin_sum: bfloat16 [96000, 256], P('seq')
All inputs are finite; a program needn't handle non-finite values.
Results may differ from a plain program's by a relative error of at most 0.014.
Values may be sent and summed in bfloat16 or wider, within the bound.
No kernel may reach another device: no remote copies, remote signals or barrier semaphores. Data moves between devices by JAX's collectives and lax.ppermute only.
A program may use at most 128 MiB of HBM per device.

v0:
```python
import jax
import jax.numpy as jnp
from jax import lax
from jax.sharding import PartitionSpec as P

HEADS = 8
HD = 32
K = 250


def in_order(blocks, dim):
    lengths = list(blocks.shape[1:])
    lengths[dim] *= blocks.shape[0]
    return jnp.moveaxis(blocks, 0, dim).reshape(lengths)


def gather_together(arrays, axis, dims):
    vector = jnp.concatenate([a.reshape(-1) for a in arrays])
    lines, at, done = (lax.all_gather(vector, axis), 0, [])
    for a, dim in zip(arrays, dims):
        blocks = lines[:, at : at + a.size].reshape(-1, *a.shape)
        done.append(in_order(blocks, dim))
        at += a.size
    return tuple(done)


def passed_along(shard, axis, by):
    peers = lax.axis_size(axis)
    pairs = [(i, i + by) for i in range(peers) if 0 <= i + by < peers]
    return lax.ppermute(shard, axis, pairs)


def layer_norm(values):
    values = values.astype(jnp.float32)
    centre = values - jnp.mean(values, axis=-1, keepdims=True)
    spread = jnp.mean(centre * centre, axis=-1, keepdims=True)
    return (centre * lax.rsqrt(spread + 1e-05)).astype(jnp.bfloat16)


def attend(query_rows, key_rows, value_rows):
    factor = query_rows.shape[-1] ** (-0.5)
    scores = (
        jnp.einsum("bqhe,bkhe->bhqk", query_rows, key_rows, preferred_element_type=jnp.float32)
        * factor
    )
    scores = scores - jnp.max(scores, axis=-1, keepdims=True)
    weights = jnp.exp(scores)
    weights = (weights / jnp.sum(weights, axis=-1, keepdims=True)).astype(jnp.bfloat16)
    return jnp.einsum(
        "bhqk,bkhe->bqhe", weights, value_rows, preferred_element_type=jnp.float32
    ).astype(jnp.bfloat16)


def attend_rows(query_rows, key_rows, value_rows, per_step):
    blocks = query_rows.shape[0] // per_step
    stacked = tuple(
        (
            member.reshape((blocks, per_step) + member.shape[1:])
            for member in (query_rows, key_rows, value_rows)
        )
    )
    attended = lax.map(lambda pieces: attend(pieces[0], pieces[1], pieces[2]), stacked)
    return attended.reshape(query_rows.shape)


def whole_block(stream, qkv_weight, out_weight, up_weight, down_weight):
    normed = layer_norm(stream)
    projected = jnp.einsum(
        "pcd,dtj->tpcj", normed, qkv_weight, preferred_element_type=jnp.float32
    ).astype(jnp.bfloat16)
    projected = projected.reshape(3, stream.shape[0], stream.shape[1], HEADS, HD)
    attended = attend_rows(projected[0], projected[1], projected[2], 1)
    branch = jnp.einsum(
        "pche,hed->pcd",
        attended,
        out_weight.reshape(HEADS, HD, -1),
        preferred_element_type=jnp.float32,
    )
    middle = (stream.astype(jnp.float32) + branch).astype(jnp.bfloat16)
    normed = layer_norm(middle)
    hidden = jax.nn.relu(
        jnp.einsum("pcd,df->pcf", normed, up_weight, preferred_element_type=jnp.float32)
    ).astype(jnp.bfloat16)
    branch = jnp.einsum("pcf,fd->pcd", hidden, down_weight, preferred_element_type=jnp.float32)
    return (middle.astype(jnp.float32) + branch).astype(jnp.bfloat16)


def on_device(
    frames, intra_qkv, intra_out, intra_up, intra_down, inter_qkv, inter_out, inter_up, inter_down
):
    seq_count = lax.axis_size("seq")
    model_count = lax.axis_size("mp")
    intra_full = gather_together((intra_qkv, intra_out, intra_up, intra_down), "mp", (2, 0, 1, 0))
    span_count = frames.shape[0] // model_count
    own_spans = lax.dynamic_slice_in_dim(frames, lax.axis_index("mp") * span_count, span_count, 0)
    finished = whole_block(own_spans, intra_full[0], intra_full[1], intra_full[2], intra_full[3])
    stream = lax.all_gather(finished, "mp", axis=0, tiled=True)
    spread_devices = seq_count * model_count
    padded_len = (K + spread_devices - 1) // spread_devices * spread_devices
    full_weights = gather_together((inter_qkv, inter_out, inter_up, inter_down), "mp", (2, 0, 1, 0))
    per_device = padded_len // spread_devices
    arranged = jnp.pad(jnp.transpose(stream, (1, 0, 2)), ((0, padded_len - K), (0, 0), (0, 0)))
    arranged = arranged.reshape(
        seq_count, model_count, per_device, stream.shape[0], stream.shape[2]
    )
    mine = lax.dynamic_index_in_dim(arranged, lax.axis_index("mp"), 1, keepdims=False)
    mine = mine.reshape(seq_count * per_device, stream.shape[0], stream.shape[2])
    spread_rows = lax.all_to_all(mine, "seq", split_axis=0, concat_axis=1, tiled=True)
    spread_rows = whole_block(
        spread_rows, full_weights[0], full_weights[1], full_weights[2], full_weights[3]
    )
    returned = lax.all_to_all(spread_rows, "seq", split_axis=1, concat_axis=0, tiled=True)
    returned = returned.reshape(seq_count, 1, per_device, stream.shape[0], stream.shape[2])
    collected = lax.all_gather(returned, "mp", axis=1, tiled=True)
    collected = collected.reshape(padded_len, stream.shape[0], stream.shape[2])
    stream = jnp.transpose(collected[:K], (1, 0, 2))
    hop_len = K // 2
    tail_rows = stream[:, hop_len:]
    carried = passed_along(tail_rows[-1], "seq", 1)
    earlier = jnp.concatenate([carried[None], tail_rows[:-1]], axis=0)
    summed = stream[:, :hop_len].astype(jnp.float32) + earlier.astype(jnp.float32)
    return summed.astype(jnp.bfloat16).reshape(-1, stream.shape[2])


def solution(mesh):
    return jax.shard_map(
        on_device,
        mesh=mesh,
        in_specs=(
            P("seq", None, None),
            P(None, None, "mp"),
            P("mp", None),
            P(None, "mp"),
            P("mp", None),
            P(None, None, "mp"),
            P("mp", None),
            P(None, "mp"),
            P("mp", None),
        ),
        out_specs=P("seq", None),
        check_vma=False,
    )
```

profile of v0, /device:TPU:8, one launch (start us, length us, event | category | flops | bytes accessed | tf_op | source)
XLA Modules:
  0.0 260.5 jit_solution(12997414813802845133)
XLA Ops:
  17.4 20.4 %all-gather.10.cloned.1.call-done = bf16[786432]{0:T(1024)(128)(2,1)} async-done(((bf16[196608]{0:T(1024)(128)(2,1)}), bf16[786432]{0:T(1024)(128)(2,1)}) %all-gather.10.cloned.1.call-update) | async-done | bytes 1572880 | tf_op jit(solution)/shard_map/all_gather | solution.py:19
  48.4 27.5 %while.20 = (s32[]{:T(128)}, bf16[6,1,250,8,32]{2,4,3,1,0:T(8,128)(2,1)}, bf16[6,1,250,8,32]{2,4,3,1,0:T(8,128)(2,1)}, bf16[6,1,250,8,32]{2,4,3,1,0:T(8,128)(2,1...) while((s32[]{:T(128)}, bf16[6,1,250,8,32]{2,4,3,1,0:T(8,128)(2,1)}, bf16[6,1,250,8,32]{2,4,3,1,0:T(8,128)(2,1)}, ...), condition=%wide.region_5.6_spmd, body=%wide.region_2.5_spmd.sunk | while | flops 99566496 | bytes 805573 | solution.py:62
  50.3 2.7 %fusion.177 = bf16[6,1,250,8,32]{2,4,3,1,0:T(8,128)(2,1)} fusion(bf16[6,1,250,8,32]{2,4,3,1,0:T(8,128)(2,1)} %get-tuple-element.220, s32[]{:T(128)} %get-tuple-element.219, f32[8,250]{1,0:T(8,128)S(1)} %fusion.176, bf16[6,1,250,8,32]{2,4,3,1,0:T(8,128)(2,1)} %get-tuple-element.227, bf16[6,1,250,8,32]{2,4,3,1,0:T(8,128)(2,1)} %get-tuple-element.229, ...), kind=kOutput, calls=%fused_computation.7.clone.1 | convolution fusion | flops 66066248 | bytes 534336 | tf_op jit(solution)/shard_map/while/body/eval_jaxpr/bhqk,bkhe->bqhe/dot_general | solution.py:49
  54.9 2.7 %fusion.177 = bf16[6,1,250,8,32]{2,4,3,1,0:T(8,128)(2,1)} fusion(bf16[6,1,250,8,32]{2,4,3,1,0:T(8,128)(2,1)} %get-tuple-element.220, s32[]{:T(128)} %get-tuple-element.219, f32[8,250]{1,0:T(8,128)S(1)} %fusion.176, bf16[6,1,250,8,32]{2,4,3,1,0:T(8,128)(2,1)} %get-tuple-element.227, bf16[6,1,250,8,32]{2,4,3,1,0:T(8,128)(2,1)} %get-tuple-element.229, ...), kind=kOutput, calls=%fused_computation.7.clone.1 | convolution fusion | flops 66066248 | bytes 534336 | tf_op jit(solution)/shard_map/while/body/eval_jaxpr/bhqk,bkhe->bqhe/dot_general | solution.py:49
  59.4 2.8 %fusion.177 = bf16[6,1,250,8,32]{2,4,3,1,0:T(8,128)(2,1)} fusion(bf16[6,1,250,8,32]{2,4,3,1,0:T(8,128)(2,1)} %get-tuple-element.220, s32[]{:T(128)} %get-tuple-element.219, f32[8,250]{1,0:T(8,128)S(1)} %fusion.176, bf16[6,1,250,8,32]{2,4,3,1,0:T(8,128)(2,1)} %get-tuple-element.227, bf16[6,1,250,8,32]{2,4,3,1,0:T(8,128)(2,1)} %get-tuple-element.229, ...), kind=kOutput, calls=%fused_computation.7.clone.1 | convolution fusion | flops 66066248 | bytes 534336 | tf_op jit(solution)/shard_map/while/body/eval_jaxpr/bhqk,bkhe->bqhe/dot_general | solution.py:49
  64.1 2.8 %fusion.177 = bf16[6,1,250,8,32]{2,4,3,1,0:T(8,128)(2,1)} fusion(bf16[6,1,250,8,32]{2,4,3,1,0:T(8,128)(2,1)} %get-tuple-element.220, s32[]{:T(128)} %get-tuple-element.219, f32[8,250]{1,0:T(8,128)S(1)} %fusion.176, bf16[6,1,250,8,32]{2,4,3,1,0:T(8,128)(2,1)} %get-tuple-element.227, bf16[6,1,250,8,32]{2,4,3,1,0:T(8,128)(2,1)} %get-tuple-element.229, ...), kind=kOutput, calls=%fused_computation.7.clone.1 | convolution fusion | flops 66066248 | bytes 534336 | tf_op jit(solution)/shard_map/while/body/eval_jaxpr/bhqk,bkhe->bqhe/dot_general | solution.py:49
  68.7 2.7 %fusion.177 = bf16[6,1,250,8,32]{2,4,3,1,0:T(8,128)(2,1)} fusion(bf16[6,1,250,8,32]{2,4,3,1,0:T(8,128)(2,1)} %get-tuple-element.220, s32[]{:T(128)} %get-tuple-element.219, f32[8,250]{1,0:T(8,128)S(1)} %fusion.176, bf16[6,1,250,8,32]{2,4,3,1,0:T(8,128)(2,1)} %get-tuple-element.227, bf16[6,1,250,8,32]{2,4,3,1,0:T(8,128)(2,1)} %get-tuple-element.229, ...), kind=kOutput, calls=%fused_computation.7.clone.1 | convolution fusion | flops 66066248 | bytes 534336 | tf_op jit(solution)/shard_map/while/body/eval_jaxpr/bhqk,bkhe->bqhe/dot_general | solution.py:49
  73.2 2.7 %fusion.177 = bf16[6,1,250,8,32]{2,4,3,1,0:T(8,128)(2,1)} fusion(bf16[6,1,250,8,32]{2,4,3,1,0:T(8,128)(2,1)} %get-tuple-element.220, s32[]{:T(128)} %get-tuple-element.219, f32[8,250]{1,0:T(8,128)S(1)} %fusion.176, bf16[6,1,250,8,32]{2,4,3,1,0:T(8,128)(2,1)} %get-tuple-element.227, bf16[6,1,250,8,32]{2,4,3,1,0:T(8,128)(2,1)} %get-tuple-element.229, ...), kind=kOutput, calls=%fused_computation.7.clone.1 | convolution fusion | flops 66066248 | bytes 534336 | tf_op jit(solution)/shard_map/while/body/eval_jaxpr/bhqk,bkhe->bqhe/dot_general | solution.py:49
  78.2 2.8 %fusion.105 = bf16[6,250,256]{2,1,0:T(8,128)(2,1)} fusion(bf16[6,250,256]{2,1,0:T(8,128)(2,1)S(1)} %get-tuple-element.144, bf16[1024,256,1]{1,0,2:T(8,128)(2,1)S(1)} %copy-done.10, bf16[256,1024,1]{0,1,2:T(8,128)(2,1)S(1)} %bitcast.240, f32[6,250]{1,0:T(8,128)S(1)} %add_rsqrt_fusion.1, f32[6,250]{1,0:T(8,128)S(1)} %broadcast_multiply_fusion.1), kind=kOutput, calls=%fused_computation.87 | convolution fusion | flops 1578624000 | bytes 2596576 | tf_op jit(solution)/shard_map/pcf,fd->pcd/dot_general | solution.py:84
  81.1 3.1 %reshape.243 = bf16[4,196608]{1,0:T(4,128)(2,1)} reshape(bf16[786432]{0:T(1024)(128)(2,1)} %all-gather.12.cloned.1.call-done) | data formatting | bytes 3145728 | tf_op jit(solution)/shard_map/all_gather | solution.py:19
  84.3 28.9 %all-gather.8.cloned.1.call-done = bf16[24,250,256]{2,1,0:T(8,128)(2,1)} async-done(((bf16[6,250,256]{2,1,0:T(8,128)(2,1)}), bf16[24,250,256]{2,1,0:T(8,128)(2,1)}) %all-gather.8.cloned.1.call-update) | async-done | bytes 3072016 | tf_op jit(solution)/shard_map/all_gather | solution.py:97
  115.3 3.2 %reshape.225 = bf16[32,4,2,24,256]{4,2,1,0,3:T(2,128)(2,1)} reshape(bf16[256,24,256]{2,0,1:T(8,128)(2,1)S(1)} %pad.4) | data formatting | bytes 6291456 | tf_op jit(solution)/shard_map/reshape | solution.py:103
  121.9 7.5 %all-to-all-start = ((bf16[64,24,256]{2,1,0:T(8,128)(2,1)}), bf16[64,24,256]{2,1,0:T(8,128)(2,1)S(1)}, u32[]{:S(2)}, u32[]{:S(2)}) async-start(bf16[64,24,256]{2,1,0:T(8,128)(2,1)} %bitcast.31), calls=%async_computation | async-start | bytes 1572864 | tf_op jit(solution)/shard_map/all_to_all | solution.py:108
  134.8 7.5 %all-to-all-done = bf16[64,24,256]{2,1,0:T(8,128)(2,1)S(1)} async-done(((bf16[64,24,256]{2,1,0:T(8,128)(2,1)}), bf16[64,24,256]{2,1,0:T(8,128)(2,1)S(1)}, u32[]{:S(2)}, u32[]{:S(2)}) %all-to-all-start) | async-done | bytes 786464 | tf_op jit(solution)/shard_map/all_to_all | solution.py:108
  144.8 36.6 %while.21 = (s32[]{:T(128)}, bf16[2,1,768,8,32]{2,4,3,1,0:T(8,128)(2,1)}, bf16[2,1,768,8,32]{2,4,3,1,0:T(8,128)(2,1)S(1)}, bf16[2,1,768,8,32]{2,4,3,1,0:T(8,128)...) while((s32[]{:T(128)}, bf16[2,1,768,8,32]{2,4,3,1,0:T(8,128)(2,1)}, ...), condition=%wide.region_13.14_spmd, body=%wide.region_10.13_spmd.sunk | while | flops 627770112 | bytes 39372868 | solution.py:62
  144.8 9.4 %fusion.181 = (f32[8,768]{1,0:T(8,128)S(1)}, f32[8,768,768]{1,2,0:T(8,128)}) fusion(bf16[2,1,768,8,32]{2,4,3,1,0:T(8,128)(2,1)S(1)} %get-tuple-element.247, s32[]{:T(128)} %get-tuple-element.237, bf16[2,1,768,8,32]{2,4,3,1,0:T(8,128)(2,1)S(1)} %get-tuple-element.246), kind=kOutput, calls=%fused_computation.123.clone.1 | convolution fusion | flops 316146432 | bytes 19686400 | tf_op jit(solution)/shard_map/while/body/eval_jaxpr/sub | solution.py:46
  154.2 8.8 %fusion.182 = bf16[2,1,768,8,32]{2,4,3,1,0:T(8,128)(2,1)} fusion(bf16[2,1,768,8,32]{2,4,3,1,0:T(8,128)(2,1)} %get-tuple-element.238, s32[]{:T(128)} %get-tuple-element.237, f32[8,768,768]{1,2,0:T(8,128)} %get-tuple-element.211, f32[8,768]{1,0:T(8,128)S(1)} %get-tuple-element.212, bf16[2,1,768,8,32]{2,4,3,1,0:T(8,128)(2,1)S(1)} %get-tuple-element.245), kind=kOutput, calls=%fused_computation.37.clone.1 | convolution fusion | flops 311623680 | bytes 19686400 | tf_op jit(solution)/shard_map/while/body/eval_jaxpr/bhqk,bkhe->bqhe/dot_general | solution.py:49
  163.1 9.4 %fusion.181 = (f32[8,768]{1,0:T(8,128)S(1)}, f32[8,768,768]{1,2,0:T(8,128)}) fusion(bf16[2,1,768,8,32]{2,4,3,1,0:T(8,128)(2,1)S(1)} %get-tuple-element.247, s32[]{:T(128)} %get-tuple-element.237, bf16[2,1,768,8,32]{2,4,3,1,0:T(8,128)(2,1)S(1)} %get-tuple-element.246), kind=kOutput, calls=%fused_computation.123.clone.1 | convolution fusion | flops 316146432 | bytes 19686400 | tf_op jit(solution)/shard_map/while/body/eval_jaxpr/sub | solution.py:46
  172.5 8.9 %fusion.182 = bf16[2,1,768,8,32]{2,4,3,1,0:T(8,128)(2,1)} fusion(bf16[2,1,768,8,32]{2,4,3,1,0:T(8,128)(2,1)} %get-tuple-element.238, s32[]{:T(128)} %get-tuple-element.237, f32[8,768,768]{1,2,0:T(8,128)} %get-tuple-element.211, f32[8,768]{1,0:T(8,128)S(1)} %get-tuple-element.212, bf16[2,1,768,8,32]{2,4,3,1,0:T(8,128)(2,1)S(1)} %get-tuple-element.245), kind=kOutput, calls=%fused_computation.37.clone.1 | convolution fusion | flops 311623680 | bytes 19686400 | tf_op jit(solution)/shard_map/while/body/eval_jaxpr/bhqk,bkhe->bqhe/dot_general | solution.py:49
  186.6 17.8 %all_to_all.24 = bf16[2,768,256]{2,0,1:T(2,128)(2,1)S(1)} all-to-all(bf16[2,768,256]{2,0,1:T(2,128)(2,1)S(1)} %copy.119), channel_id=1, replica_groups=mesh['seq'=32,'mp'=4] {'seq'}, dimensions={1} | all-to-all | bytes 1572864 | tf_op jit(solution)/shard_map/all_to_all | solution.py:112
  205.4 31.4 %all-gather.14.cloned.1.call-done = bf16[32,8,24,256]{3,2,0,1:T(8,128)(2,1)} async-done(((bf16[32,2,24,256]{3,2,0,1:T(8,128)(2,1)}), bf16[32,8,24,256]{3,2,0,1:T(8,128)(2,1)}) %all-gather.14.cloned.1.call-update) | async-done | bytes 3145744 | tf_op jit(solution)/shard_map/all_gather | solution.py:114
  239.5 2.6 collective-permute-start
  242.1 6.5 %collective-permute-done = bf16[125,256]{1,0:T(8,128)(2,1)S(1)} collective-permute-done((bf16[125,256]{1,0:T(8,128)(2,1)S(1)}, bf16[125,256]{1,0:T(8,128)(2,1)S(1)}, u32[]{:S(2)}, u32[]{:S(2)}) %collective-permute-start) | collective-permute-done | bytes 64032 | tf_op jit(solution)/shard_map/ppermute | solution.py:30
  251.3 2.7 %reshape.238 = bf16[3000,256]{1,0:T(8,128)(2,1)} reshape(bf16[24,125,256]{2,1,0:T(8,128)(2,1)} %copy.123) | data formatting | bytes 3072000 | tf_op jit(solution)/shard_map/reshape | solution.py:122
  (115 shorter events, 59.4 us)
Async XLA Ops:
  6.5 9.1 %copy-start = (bf16[24,250,256]{2,0,1:T(8,128)(2,1)S(1)}, bf16[24,250,256]{2,0,1:T(8,128)(2,1)}, u32[]{:S(2)}) copy-start(bf16[24,250,256]{2,0,1:T(8,128)(2,1)} %param.13) | copy-start | bytes 9216004
  6.5 5.1 %copy-start.11 = (bf16[256,3,64]{0,2,1:T(8,128)(2,1)S(1)}, bf16[256,3,64]{0,2,1:T(8,128)(2,1)}, u32[]{:S(2)}) copy-start(bf16[256,3,64]{0,2,1:T(8,128)(2,1)} %param.18) | copy-start | bytes 294916
  6.5 31.3 %all-gather.10.cloned.1.call-start = ((), (), s32[]{:S(2)}) async-start(), calls=%async_computation.3 | async-start | bytes 1966080 | tf_op jit(solution)/shard_map/all_gather | solution.py:19
  11.5 69.6 %all-gather.12.cloned.1.call-start = ((), (), s32[]{:S(2)}) async-start(), calls=%async_computation.4 | async-start | bytes 1966080 | tf_op jit(solution)/shard_map/all_gather | solution.py:19
  15.6 97.6 %all-gather.8.cloned.1.call-start = ((), (), s32[]{:S(2)}) async-start(), calls=%async_computation.2 | async-start | bytes 3932160 | tf_op jit(solution)/shard_map/all_gather | solution.py:97
  15.9 1.0 copy-start.2
  39.8 1.4 copy-start.5
  41.2 3.2 %copy-start.3 = (bf16[6,250,256]{2,0,1:T(8,128)(2,1)S(1)}, bf16[6,250,256]{2,0,1:T(8,128)(2,1)}, u32[]{:S(2)}) copy-start(bf16[6,250,256]{2,0,1:T(8,128)(2,1)} %copy-done.2) | copy-start | bytes 2304004
  45.4 1.5 slice-start.2
  45.4 1.6 copy-start.6
  76.0 2.3 copy-start.10
  120.3 9.3 %copy-start.4 = (bf16[4,196608]{1,0:T(4,128)(2,1)S(1)}, bf16[4,196608]{1,0:T(4,128)(2,1)}, u32[]{:S(2)}) copy-start(bf16[4,196608]{1,0:T(4,128)(2,1)} %reshape.243) | copy-start | bytes 4718596
  121.9 20.4 %all-to-all-start = ((bf16[64,24,256]{2,1,0:T(8,128)(2,1)}), bf16[64,24,256]{2,1,0:T(8,128)(2,1)S(1)}, u32[]{:S(2)}, u32[]{:S(2)}) async-start(bf16[64,24,256]{2,1,0:T(8,128)(2,1)} %bitcast.31), calls=%async_computation | async-start | bytes 1572864 | tf_op jit(solution)/shard_map/all_to_all | solution.py:108
  129.4 1.4 slice-start
  129.4 107.4 %all-gather.14.cloned.1.call-start = ((), (), s32[]{:S(2)}) async-start(), calls=%async_computation.5 | async-start | bytes 3932160 | tf_op jit(solution)/shard_map/all_gather | solution.py:114
  130.8 1.3 slice-start.1
  131.5 1.1 copy-start.7
  182.2 1.9 copy-start.8
  182.2 1.9 copy-start.9
  239.5 9.2 %collective-permute-start = (bf16[125,256]{1,0:T(8,128)(2,1)S(1)}, bf16[125,256]{1,0:T(8,128)(2,1)S(1)}, u32[]{:S(2)}, u32[]{:S(2)}) collective-permute-start(bf16[125,256]{1,0:T(8,128)(2,1)S(1)} %bitcast.251), channel_id=1, source_target_pairs={{0,4},{4,8},{8,12},{12,16},{16,20},{20,24},{24,28},{28,32},{32,36}... | collective-permute-start | bytes 192008 | tf_op jit(solution)/shard_map/ppermute | solution.py:30
  249.8 4.2 %copy-start.1 = (bf16[24,250,256]{2,0,1:T(8,128)(2,1)S(1)}, bf16[24,250,256]{2,0,1:T(8,128)(2,1)}, u32[]{:S(2)}) copy-start(bf16[24,250,256]{2,0,1:T(8,128)(2,1)} %param.13) | copy-start | bytes 9216004
Sparse Core Ops, SparseCore 0:
  11.7 26.1 all-gather.9
  39.5 23.1 all-gather.11
  81.2 31.9 all-gather.7
  205.6 31.2 all-gather.13
where the time goes:
time: 262 us; the launch traced here: 261 us
  waiting for transfers between devices  94.7 us (36%)
  matrix products  73.9 us (28%)
  local copies, waits for them, and re-layouts  44.2 us (17%)
  blocking collectives  17.8 us (7%)
  between operations  13.7 us (5%)
  starting transfers between devices  10.4 us (4%)
  other arithmetic  5.78 us (2%)
    dot_general x8, matrix products, attend(): jnp.einsum('bhqk,bkhe->bqhe', weights, value_rows, preferred_element_type...  34.2 us
    all_gather x1, waiting for transfers between devices, on_device(): collected = lax.all_gather(returned, 'mp', axis=1, tiled=True)  31.4 us
    sub x8, matrix products, attend(): scores = scores - jnp.max(scores, axis=-1, keepdims=True)  29.9 us
    all_gather x1, waiting for transfers between devices, on_device(): stream = lax.all_gather(finished, 'mp', axis=0, tiled=True)  28.9 us
    all_gather x2, waiting for transfers between devices, gather_together(): lines, at, done = (lax.all_gather(vector, axis), 0, [])  20.4 us
    all_to_all x1, blocking collectives, on_device(): lax.all_to_all(spread_rows, 'seq', split_axis=1, concat_axis=0, tiled=True)  17.8 us
    unnamed x36, local copies, waits for them, and re-layouts  9.77 us
    all_to_all x1, starting transfers between devices, on_device(): lax.all_to_all(mine, 'seq', split_axis=0, concat_axis=1, tiled=True)  7.49 us
  transfers between devices with their start and end apart: 6, of which 5 were waited for; matrix products, arithmetic and copies ran while one was open for 22% of the time, Pallas kernels for 0%

commit v1 on v0

--- a/solution.py
+++ b/solution.py
@@ -111,7 +111,9 @@
     )
     returned = lax.all_to_all(spread_rows, "seq", split_axis=1, concat_axis=0, tiled=True)
     returned = returned.reshape(seq_count, 1, per_device, stream.shape[0], stream.shape[2])
-    collected = lax.all_gather(returned, "mp", axis=1, tiled=True)
+    collected = jnp.concatenate(
+        lax.all_to_all(jnp.stack([returned] * lax.axis_size("mp")), "mp", 0, 0), axis=1
+    )
     collected = collected.reshape(padded_len, stream.shape[0], stream.shape[2])
     stream = jnp.transpose(collected[:K], (1, 0, 2))
     hop_len = K // 2

time: 262 us -> 276 us (1.053)
  blocking collectives: 17.8 us -> 59.2 us
  waiting for transfers between devices: 94.7 us -> 63.3 us
  local copies, waits for them, and re-layouts: 44.2 us -> 48.4 us
    all_to_all x0 -> x1, blocking collectives: none -> 41.4 us  [on_device(): lax.all_to_all(jnp.stack([returned] * lax.axis_size('mp')), 'mp', 0, 0)]
    all_gather x1 -> x0, waiting for transfers between devices: 31.4 us -> none  [on_device(): collected = lax.all_gather(returned, 'mp', axis=1, tiled=True)]
    all_to_all x0 -> x1, local copies, waits for them, and re-layouts: none -> 3.39 us  [on_device(): lax.all_to_all(jnp.stack([returned] * lax.axis_size('mp')), 'mp', 0, 0)]
    another operation x0 -> x1, local copies, waits for them, and re-layouts: none -> 3.1 us  [on_device(): jnp.stack([returned] * lax.axis_size('mp'))]
  transfers between devices with their start and end apart: 6 -> 5, of which waited for: 5 -> 4; matrix products, arithmetic and copies ran while one was open for 22% -> 20% of each run, Pallas kernels for 0% -> 0%
where the time goes in v1:
time: 276 us; the launch traced here: 275 us
  matrix products  74 us (27%)
  waiting for transfers between devices  63.3 us (23%)
  blocking collectives  59.2 us (21%)
  local copies, waits for them, and re-layouts  48.4 us (18%)
  between operations  13.7 us (5%)
  starting transfers between devices  10.4 us (4%)
  other arithmetic  5.78 us (2%)
    all_to_all x1, blocking collectives, on_device(): lax.all_to_all(jnp.stack([returned] * lax.axis_size('mp')), 'mp', 0, 0)  41.4 us
    dot_general x8, matrix products, attend(): jnp.einsum('bhqk,bkhe->bqhe', weights, value_rows, preferred_element_type...  34.2 us
    sub x8, matrix products, attend(): scores = scores - jnp.max(scores, axis=-1, keepdims=True)  29.9 us
    all_gather x1, waiting for transfers between devices, on_device(): stream = lax.all_gather(finished, 'mp', axis=0, tiled=True)  28.9 us
    all_gather x2, waiting for transfers between devices, gather_together(): lines, at, done = (lax.all_gather(vector, axis), 0, [])  20.4 us
    all_to_all x1, blocking collectives, on_device(): lax.all_to_all(spread_rows, 'seq', split_axis=1, concat_axis=0, tiled=True)  17.8 us
    unnamed x36, local copies, waits for them, and re-layouts  9.76 us
    all_to_all x1, waiting for transfers between devices, on_device(): lax.all_to_all(mine, 'seq', split_axis=0, concat_axis=1, tiled=True)  7.66 us
  transfers between devices with their start and end apart: 5, of which 4 were waited for; matrix products, arithmetic and copies ran while one was open for 20% of the time, Pallas kernels for 0%

profile of v1, /device:TPU:8, one launch (start us, length us, event | category | flops | bytes accessed | tf_op | source)
XLA Modules:
  0.0 274.8 jit_solution(2454683857177244326)
XLA Ops:
  17.4 20.4 %all-gather.8.cloned.1.call-done = bf16[786432]{0:T(1024)(128)(2,1)} async-done(((bf16[196608]{0:T(1024)(128)(2,1)}), bf16[786432]{0:T(1024)(128)(2,1)}) %all-gather.8.cloned.1.call-update) | async-done | bytes 1572880 | tf_op jit(solution)/shard_map/all_gather | solution.py:19
  48.4 27.6 %while.20 = (s32[]{:T(128)}, bf16[6,1,250,8,32]{2,4,3,1,0:T(8,128)(2,1)}, bf16[6,1,250,8,32]{2,4,3,1,0:T(8,128)(2,1)}, bf16[6,1,250,8,32]{2,4,3,1,0:T(8,128)(2,1...) while((s32[]{:T(128)}, bf16[6,1,250,8,32]{2,4,3,1,0:T(8,128)(2,1)}, bf16[6,1,250,8,32]{2,4,3,1,0:T(8,128)(2,1)}, ...), condition=%wide.region_5.6_spmd, body=%wide.region_2.5_spmd.sunk | while | flops 99566496 | bytes 805573 | solution.py:62
  50.3 2.8 %fusion.177 = bf16[6,1,250,8,32]{2,4,3,1,0:T(8,128)(2,1)} fusion(bf16[6,1,250,8,32]{2,4,3,1,0:T(8,128)(2,1)} %get-tuple-element.240, s32[]{:T(128)} %get-tuple-element.239, f32[8,250]{1,0:T(8,128)S(1)} %fusion.176, bf16[6,1,250,8,32]{2,4,3,1,0:T(8,128)(2,1)} %get-tuple-element.247, bf16[6,1,250,8,32]{2,4,3,1,0:T(8,128)(2,1)} %get-tuple-element.249, ...), kind=kOutput, calls=%fused_computation.7.clone.1 | convolution fusion | flops 66066248 | bytes 534336 | tf_op jit(solution)/shard_map/while/body/eval_jaxpr/bhqk,bkhe->bqhe/dot_general | solution.py:49
  54.9 2.8 %fusion.177 = bf16[6,1,250,8,32]{2,4,3,1,0:T(8,128)(2,1)} fusion(bf16[6,1,250,8,32]{2,4,3,1,0:T(8,128)(2,1)} %get-tuple-element.240, s32[]{:T(128)} %get-tuple-element.239, f32[8,250]{1,0:T(8,128)S(1)} %fusion.176, bf16[6,1,250,8,32]{2,4,3,1,0:T(8,128)(2,1)} %get-tuple-element.247, bf16[6,1,250,8,32]{2,4,3,1,0:T(8,128)(2,1)} %get-tuple-element.249, ...), kind=kOutput, calls=%fused_computation.7.clone.1 | convolution fusion | flops 66066248 | bytes 534336 | tf_op jit(solution)/shard_map/while/body/eval_jaxpr/bhqk,bkhe->bqhe/dot_general | solution.py:49
  59.5 2.8 %fusion.177 = bf16[6,1,250,8,32]{2,4,3,1,0:T(8,128)(2,1)} fusion(bf16[6,1,250,8,32]{2,4,3,1,0:T(8,128)(2,1)} %get-tuple-element.240, s32[]{:T(128)} %get-tuple-element.239, f32[8,250]{1,0:T(8,128)S(1)} %fusion.176, bf16[6,1,250,8,32]{2,4,3,1,0:T(8,128)(2,1)} %get-tuple-element.247, bf16[6,1,250,8,32]{2,4,3,1,0:T(8,128)(2,1)} %get-tuple-element.249, ...), kind=kOutput, calls=%fused_computation.7.clone.1 | convolution fusion | flops 66066248 | bytes 534336 | tf_op jit(solution)/shard_map/while/body/eval_jaxpr/bhqk,bkhe->bqhe/dot_general | solution.py:49
  64.1 2.8 %fusion.177 = bf16[6,1,250,8,32]{2,4,3,1,0:T(8,128)(2,1)} fusion(bf16[6,1,250,8,32]{2,4,3,1,0:T(8,128)(2,1)} %get-tuple-element.240, s32[]{:T(128)} %get-tuple-element.239, f32[8,250]{1,0:T(8,128)S(1)} %fusion.176, bf16[6,1,250,8,32]{2,4,3,1,0:T(8,128)(2,1)} %get-tuple-element.247, bf16[6,1,250,8,32]{2,4,3,1,0:T(8,128)(2,1)} %get-tuple-element.249, ...), kind=kOutput, calls=%fused_computation.7.clone.1 | convolution fusion | flops 66066248 | bytes 534336 | tf_op jit(solution)/shard_map/while/body/eval_jaxpr/bhqk,bkhe->bqhe/dot_general | solution.py:49
  73.3 2.8 %fusion.177 = bf16[6,1,250,8,32]{2,4,3,1,0:T(8,128)(2,1)} fusion(bf16[6,1,250,8,32]{2,4,3,1,0:T(8,128)(2,1)} %get-tuple-element.240, s32[]{:T(128)} %get-tuple-element.239, f32[8,250]{1,0:T(8,128)S(1)} %fusion.176, bf16[6,1,250,8,32]{2,4,3,1,0:T(8,128)(2,1)} %get-tuple-element.247, bf16[6,1,250,8,32]{2,4,3,1,0:T(8,128)(2,1)} %get-tuple-element.249, ...), kind=kOutput, calls=%fused_computation.7.clone.1 | convolution fusion | flops 66066248 | bytes 534336 | tf_op jit(solution)/shard_map/while/body/eval_jaxpr/bhqk,bkhe->bqhe/dot_general | solution.py:49
  78.3 2.8 %fusion.105 = bf16[6,250,256]{2,1,0:T(8,128)(2,1)} fusion(bf16[6,250,256]{2,1,0:T(8,128)(2,1)S(1)} %get-tuple-element.164, bf16[1024,256,1]{1,0,2:T(8,128)(2,1)S(1)} %copy-done.10, bf16[256,1024,1]{0,1,2:T(8,128)(2,1)S(1)} %bitcast.242, f32[6,250]{1,0:T(8,128)S(1)} %add_rsqrt_fusion.1, f32[6,250]{1,0:T(8,128)S(1)} %broadcast_multiply_fusion.1), kind=kOutput, calls=%fused_computation.87 | convolution fusion | flops 1578624000 | bytes 2596576 | tf_op jit(solution)/shard_map/pcf,fd->pcd/dot_general | solution.py:84
  81.2 3.2 %reshape.241 = bf16[4,196608]{1,0:T(4,128)(2,1)} reshape(bf16[786432]{0:T(1024)(128)(2,1)} %all-gather.10.cloned.1.call-done) | data formatting | bytes 3145728 | tf_op jit(solution)/shard_map/all_gather | solution.py:19
  84.4 28.9 %all-gather.6.cloned.1.call-done = bf16[24,250,256]{2,1,0:T(8,128)(2,1)} async-done(((bf16[6,250,256]{2,1,0:T(8,128)(2,1)}), bf16[24,250,256]{2,1,0:T(8,128)(2,1)}) %all-gather.6.cloned.1.call-update) | async-done | bytes 3072016 | tf_op jit(solution)/shard_map/all_gather | solution.py:97
  115.4 3.2 %reshape.224 = bf16[32,4,2,24,256]{4,2,1,0,3:T(2,128)(2,1)} reshape(bf16[256,24,256]{2,0,1:T(8,128)(2,1)S(1)} %pad.4) | data formatting | bytes 6291456 | tf_op jit(solution)/shard_map/reshape | solution.py:103
  121.9 7.5 %all-to-all-start = ((bf16[64,24,256]{2,1,0:T(8,128)(2,1)}), bf16[64,24,256]{2,1,0:T(8,128)(2,1)S(1)}, u32[]{:S(2)}, u32[]{:S(2)}) async-start(bf16[64,24,256]{2,1,0:T(8,128)(2,1)} %bitcast.31), calls=%async_computation | async-start | bytes 1572864 | tf_op jit(solution)/shard_map/all_to_all | solution.py:108
  134.7 7.7 %all-to-all-done = bf16[64,24,256]{2,1,0:T(8,128)(2,1)S(1)} async-done(((bf16[64,24,256]{2,1,0:T(8,128)(2,1)}), bf16[64,24,256]{2,1,0:T(8,128)(2,1)S(1)}, u32[]{:S(2)}, u32[]{:S(2)}) %all-to-all-start) | async-done | bytes 786464 | tf_op jit(solution)/shard_map/all_to_all | solution.py:108
  144.8 36.6 %while.21 = (s32[]{:T(128)}, bf16[2,1,768,8,32]{2,4,3,1,0:T(8,128)(2,1)}, bf16[2,1,768,8,32]{2,4,3,1,0:T(8,128)(2,1)S(1)}, bf16[2,1,768,8,32]{2,4,3,1,0:T(8,128)...) while((s32[]{:T(128)}, bf16[2,1,768,8,32]{2,4,3,1,0:T(8,128)(2,1)}, ...), condition=%wide.region_13.14_spmd, body=%wide.region_10.13_spmd.sunk | while | flops 627770112 | bytes 39372868 | solution.py:62
  144.9 9.5 %fusion.181 = (f32[8,768]{1,0:T(8,128)S(1)}, f32[8,768,768]{1,2,0:T(8,128)}) fusion(bf16[2,1,768,8,32]{2,4,3,1,0:T(8,128)(2,1)S(1)} %get-tuple-element.267, s32[]{:T(128)} %get-tuple-element.257, bf16[2,1,768,8,32]{2,4,3,1,0:T(8,128)(2,1)S(1)} %get-tuple-element.266), kind=kOutput, calls=%fused_computation.123.clone.1 | convolution fusion | flops 316146432 | bytes 19686400 | tf_op jit(solution)/shard_map/while/body/eval_jaxpr/sub | solution.py:46
  154.3 8.9 %fusion.182 = bf16[2,1,768,8,32]{2,4,3,1,0:T(8,128)(2,1)} fusion(bf16[2,1,768,8,32]{2,4,3,1,0:T(8,128)(2,1)} %get-tuple-element.258, s32[]{:T(128)} %get-tuple-element.257, f32[8,768,768]{1,2,0:T(8,128)} %get-tuple-element.231, f32[8,768]{1,0:T(8,128)S(1)} %get-tuple-element.232, bf16[2,1,768,8,32]{2,4,3,1,0:T(8,128)(2,1)S(1)} %get-tuple-element.265), kind=kOutput, calls=%fused_computation.37.clone.1 | convolution fusion | flops 311623680 | bytes 19686400 | tf_op jit(solution)/shard_map/while/body/eval_jaxpr/bhqk,bkhe->bqhe/dot_general | solution.py:49
  163.2 9.4 %fusion.181 = (f32[8,768]{1,0:T(8,128)S(1)}, f32[8,768,768]{1,2,0:T(8,128)}) fusion(bf16[2,1,768,8,32]{2,4,3,1,0:T(8,128)(2,1)S(1)} %get-tuple-element.267, s32[]{:T(128)} %get-tuple-element.257, bf16[2,1,768,8,32]{2,4,3,1,0:T(8,128)(2,1)S(1)} %get-tuple-element.266), kind=kOutput, calls=%fused_computation.123.clone.1 | convolution fusion | flops 316146432 | bytes 19686400 | tf_op jit(solution)/shard_map/while/body/eval_jaxpr/sub | solution.py:46
  172.6 8.9 %fusion.182 = bf16[2,1,768,8,32]{2,4,3,1,0:T(8,128)(2,1)} fusion(bf16[2,1,768,8,32]{2,4,3,1,0:T(8,128)(2,1)} %get-tuple-element.258, s32[]{:T(128)} %get-tuple-element.257, f32[8,768,768]{1,2,0:T(8,128)} %get-tuple-element.231, f32[8,768]{1,0:T(8,128)S(1)} %get-tuple-element.232, bf16[2,1,768,8,32]{2,4,3,1,0:T(8,128)(2,1)S(1)} %get-tuple-element.265), kind=kOutput, calls=%fused_computation.37.clone.1 | convolution fusion | flops 311623680 | bytes 19686400 | tf_op jit(solution)/shard_map/while/body/eval_jaxpr/bhqk,bkhe->bqhe/dot_general | solution.py:49
  186.8 17.8 %all_to_all.29 = bf16[2,768,256]{2,0,1:T(2,128)(2,1)S(1)} all-to-all(bf16[2,768,256]{2,0,1:T(2,128)(2,1)S(1)} %copy.173), channel_id=1, replica_groups=mesh['seq'=32,'mp'=4] {'seq'}, dimensions={1} | all-to-all | bytes 1572864 | tf_op jit(solution)/shard_map/all_to_all | solution.py:112
  205.5 3.1 %stack.3 = bf16[4,32,1,2,24,256]{5,3,1,4,2,0:T(2,128)(2,1)S(1)} broadcast(bf16[32,2,24,256]{3,1,0,2:T(2,128)(2,1)S(1)} %copy.175), dimensions={1,3,4,5} | broadcast | bytes 3932160 | tf_op jit(solution)/shard_map/stack | solution.py:115
  208.6 41.4 %all_to_all.30 = bf16[4,32,1,2,24,256]{5,3,1,4,2,0:T(2,128)(2,1)S(1)} all-to-all(bf16[4,32,1,2,24,256]{5,3,1,4,2,0:T(2,128)(2,1)S(1)} %stack.3), channel_id=1, replica_groups=mesh['seq'=32,'mp'=4] {'mp'}, dimensions={0} | all-to-all | bytes 6291456 | tf_op jit(solution)/shard_map/all_to_all | solution.py:115
  250.0 3.4 %copy.176 = bf16[4,32,1,2,24,256]{5,4,3,0,1,2:T(8,128)(2,1)S(1)} copy(bf16[4,32,1,2,24,256]{5,3,1,4,2,0:T(2,128)(2,1)S(1)} %all_to_all.30) | data formatting | bytes 6291456 | tf_op jit(solution)/shard_map/all_to_all | solution.py:115
  253.8 2.8 %collective-permute-start = (bf16[125,256]{1,0:T(8,128)(2,1)S(1)}, bf16[125,256]{1,0:T(8,128)(2,1)S(1)}, u32[]{:S(2)}, u32[]{:S(2)}) collective-permute-start(bf16[125,256]{1,0:T(8,128)(2,1)S(1)} %bitcast.253), channel_id=1, source_target_pairs={{0,4},{4,8},{8,12},{12,16},{16,20},{20,24},{24,28},{28,32},{32,36}... | collective-permute-start | bytes 192008 | tf_op jit(solution)/shard_map/ppermute | solution.py:30
  256.7 6.2 %collective-permute-done = bf16[125,256]{1,0:T(8,128)(2,1)S(1)} collective-permute-done((bf16[125,256]{1,0:T(8,128)(2,1)S(1)}, bf16[125,256]{1,0:T(8,128)(2,1)S(1)}, u32[]{:S(2)}, u32[]{:S(2)}) %collective-permute-start) | collective-permute-done | bytes 64032 | tf_op jit(solution)/shard_map/ppermute | solution.py:30
  (115 shorter events, 62.3 us)
Async XLA Ops:
  6.5 9.1 %copy-start = (bf16[24,250,256]{2,0,1:T(8,128)(2,1)S(1)}, bf16[24,250,256]{2,0,1:T(8,128)(2,1)}, u32[]{:S(2)}) copy-start(bf16[24,250,256]{2,0,1:T(8,128)(2,1)} %param.13) | copy-start | bytes 9216004
  6.5 5.1 %copy-start.11 = (bf16[256,3,64]{0,2,1:T(8,128)(2,1)S(1)}, bf16[256,3,64]{0,2,1:T(8,128)(2,1)}, u32[]{:S(2)}) copy-start(bf16[256,3,64]{0,2,1:T(8,128)(2,1)} %param.18) | copy-start | bytes 294916
  6.5 31.3 %all-gather.8.cloned.1.call-start = ((), (), s32[]{:S(2)}) async-start(), calls=%async_computation.4 | async-start | bytes 1966080 | tf_op jit(solution)/shard_map/all_gather | solution.py:19
  11.5 69.7 %all-gather.10.cloned.1.call-start = ((), (), s32[]{:S(2)}) async-start(), calls=%async_computation.5 | async-start | bytes 1966080 | tf_op jit(solution)/shard_map/all_gather | solution.py:19
  15.6 97.7 %all-gather.6.cloned.1.call-start = ((), (), s32[]{:S(2)}) async-start(), calls=%async_computation.3 | async-start | bytes 3932160 | tf_op jit(solution)/shard_map/all_gather | solution.py:97
  15.9 1.0 copy-start.2
  39.8 1.4 copy-start.5
  41.2 3.2 %copy-start.3 = (bf16[6,250,256]{2,0,1:T(8,128)(2,1)S(1)}, bf16[6,250,256]{2,0,1:T(8,128)(2,1)}, u32[]{:S(2)}) copy-start(bf16[6,250,256]{2,0,1:T(8,128)(2,1)} %copy-done.2) | copy-start | bytes 2304004
  45.4 1.5 slice-start.2
  45.4 1.6 copy-start.6
  76.0 2.3 copy-start.10
  120.4 9.1 %copy-start.4 = (bf16[4,196608]{1,0:T(4,128)(2,1)S(1)}, bf16[4,196608]{1,0:T(4,128)(2,1)}, u32[]{:S(2)}) copy-start(bf16[4,196608]{1,0:T(4,128)(2,1)} %reshape.241) | copy-start | bytes 4718596
  121.9 20.4 %all-to-all-start = ((bf16[64,24,256]{2,1,0:T(8,128)(2,1)}), bf16[64,24,256]{2,1,0:T(8,128)(2,1)S(1)}, u32[]{:S(2)}, u32[]{:S(2)}) async-start(bf16[64,24,256]{2,1,0:T(8,128)(2,1)} %bitcast.31), calls=%async_computation | async-start | bytes 1572864 | tf_op jit(solution)/shard_map/all_to_all | solution.py:108
  129.5 1.2 slice-start
  130.6 1.3 slice-start.1
  131.4 1.1 copy-start.7
  182.3 1.9 copy-start.8
  182.3 1.9 copy-start.9
  253.8 9.2 %collective-permute-start = (bf16[125,256]{1,0:T(8,128)(2,1)S(1)}, bf16[125,256]{1,0:T(8,128)(2,1)S(1)}, u32[]{:S(2)}, u32[]{:S(2)}) collective-permute-start(bf16[125,256]{1,0:T(8,128)(2,1)S(1)} %bitcast.253), channel_id=1, source_target_pairs={{0,4},{4,8},{8,12},{12,16},{16,20},{20,24},{24,28},{28,32},{32,36}... | collective-permute-start | bytes 192008 | tf_op jit(solution)/shard_map/ppermute | solution.py:30
  264.1 4.2 %copy-start.1 = (bf16[24,250,256]{2,0,1:T(8,128)(2,1)S(1)}, bf16[24,250,256]{2,0,1:T(8,128)(2,1)}, u32[]{:S(2)}) copy-start(bf16[24,250,256]{2,0,1:T(8,128)(2,1)} %param.13) | copy-start | bytes 9216004
Sparse Core Ops, SparseCore 0:
  11.7 26.1 all-gather.7
  39.5 23.0 all-gather.9
  81.3 31.9 all-gather.5
